TPU v7x, 512 devices: a whole 4x4x16 slice. The times are simulated.
512 devices in a mesh: rows: 128 (over x, z, core), cols: 4 (over y).
Axes of the slice: x: 4, y: 4, z: 16, core: 2. Of those that a mesh axis runs over, the one named last changes fastest.
Arguments:
- tiles: bfloat16 [65536, 4096], P(('rows', 'cols')), may hold values from -0.125 to 0.125
- integral_cd_tile: int32 [65536], P(('rows', 'cols')), may hold values from 0 to 511
- part_dest: int32 [16384, 1], P(('rows', 'cols')), may hold values from 0 to 127; in each aligned block of 32 rows (0 to 31, 32 to 63, ...) at most 2 rows name the same one
- partial_row_place: int32 [16384], P(('rows', 'cols')), may hold values from 0 to 15
- amplitudes: bfloat16 [4, 512, 4096], P('cols', 'rows'), may hold values from -6 to 6
- residual_in: float32 [128, 16, 4096], P('rows', 'cols'), may hold values from -6 to 6
Outputs:
- residual: float32 [128, 16, 4096], P('rows', 'cols')
Inputs may be any that keep to these rules, and one draw needn't show every extreme that they name: `part_dest`: among the 32 partial tiles of one device no index of rows is named more than 2 times, and at least one is named exactly 2 times.
All inputs are finite; a program needn't handle non-finite values.
Results may differ from a plain program's by a relative error of at most 0.0022.
Values may be sent and summed in bfloat16 or wider, within the bound.
A program may use at most 64 MiB of HBM per device.

v0:
```python
import jax
import jax.numpy as jnp
from jax import lax
from jax.sharding import PartitionSpec as P

TILE_SPAN = 64
NIJ = 64
TILES_PER_PART = 4
PAB = 32
OWNR = 16


def per_device(tiles, integral_cd_tile, part_dest, partial_row_place, amplitudes, residual_in):
    gathered = lax.all_gather(amplitudes, "rows", axis=1, tiled=True)[0]
    picked = jnp.take(gathered, integral_cd_tile, axis=0).reshape(
        PAB, TILES_PER_PART, NIJ, TILE_SPAN
    )
    block_list = tiles.reshape(PAB, TILES_PER_PART, TILE_SPAN, TILE_SPAN)
    per_tile = jnp.einsum("ptic,ptac->ptia", picked, block_list, preferred_element_type=jnp.float32)
    partial_value = jnp.sum(per_tile, axis=1)
    partial_value = partial_value.reshape(PAB, NIJ * TILE_SPAN).astype(jnp.bfloat16)
    row_count = lax.axis_size("rows")
    capacity = max(2, 2 * PAB // row_count)
    destination = part_dest[:, 0]
    onehot = (destination[:, None] == jnp.arange(row_count, dtype=jnp.int32)[None, :]).astype(
        jnp.int32
    )
    earlier = jnp.sum((jnp.cumsum(onehot, axis=0) - onehot) * onehot, axis=1)
    position = destination * capacity + earlier
    outgoing = (
        jnp.zeros((row_count * capacity, NIJ * TILE_SPAN), jnp.bfloat16)
        .at[position]
        .set(partial_value)
    )
    slot_ids = (
        jnp.full((row_count * capacity,), float(OWNR), jnp.float32)
        .at[position]
        .set(partial_row_place.astype(jnp.float32))
        .astype(jnp.bfloat16)
    )
    incoming, incoming_ids = (
        lax.all_to_all(
            outgoing.reshape(row_count, capacity, NIJ * TILE_SPAN),
            "rows",
            split_axis=0,
            concat_axis=0,
            tiled=True,
        ),
        lax.all_to_all(
            slot_ids.reshape(row_count, capacity), "rows", split_axis=0, concat_axis=0, tiled=True
        ),
    )
    incoming = incoming.reshape(row_count * capacity, NIJ * TILE_SPAN)
    incoming_ids = incoming_ids.reshape(row_count * capacity).astype(jnp.float32)
    select = (incoming_ids[None, :] == jnp.arange(OWNR, dtype=jnp.float32)[:, None]).astype(
        jnp.bfloat16
    )
    owned = jnp.dot(select, incoming, preferred_element_type=jnp.float32)
    shared = lax.psum_scatter(owned, "cols", scatter_dimension=0, tiled=True)
    return residual_in + shared[None, :, :]


def solution(mesh):
    return jax.shard_map(
        per_device,
        mesh=mesh,
        in_specs=(
            P(("rows", "cols"), None),
            P(("rows", "cols")),
            P(("rows", "cols"), None),
            P(("rows", "cols")),
            P("cols", "rows", None),
            P("rows", "cols", None),
        ),
        out_specs=P("rows", "cols", None),
        check_vma=False,
    )
```

profile of v0, /device:TPU:2, one launch (start us, length us, event | category | flops | bytes accessed | tf_op | source)
XLA Modules:
  0.0 361.6 jit_solution(1006233409174559257)
XLA Ops:
  6.5 1.4 copy.10
  8.0 0.7 convert_element_type.27
  8.7 0.7 fusion.13
  9.5 0.8 select_reduce_fusion
  10.3 0.7 fusion.16
  11.0 0.7 scatter_custom_fusion
  11.6 0.8 all_to_all.12
  12.4 19.5 %all-to-all-start = ((bf16[128,1,2]{2,1,0:T(2,128)(2,1)}), bf16[128,1,2]{2,1,0:T(2,128)(2,1)S(1)}, u32[]{:S(2)}, u32[]{:S(2)}) async-start(bf16[128,1,2]{2,1,0:T(2,128)(2,1)} %all_to_all.12), calls=%async_computation | async-start | bytes 131072 | tf_op jit(solution)/shard_map/all_to_all | solution.py:49
  32.0 3.3 reshape.37
  35.4 125.5 %all-gather.2.cloned.1.call-done = bf16[1,512,4096]{2,0,1:T(2,128)(2,1)} async-done(((bf16[1,4,4096]{2,0,1:T(2,128)(2,1)}), bf16[1,512,4096]{2,0,1:T(2,128)(2,1)}) %all-gather.2.cloned.1.call-update) | async-done | bytes 4194320 | tf_op jit(solution)/shard_map/all_gather | solution.py:14
  160.9 10.1 %copy.14 = bf16[1,512,4096]{2,1,0:T(8,128)(2,1)} copy(bf16[1,512,4096]{2,0,1:T(2,128)(2,1)} %all-gather.2.cloned.1.call-done) | data formatting | bytes 8388608
  171.0 4.9 %gather_fusion = bf16[128,4096]{1,0:T(8,128)(2,1)S(1)} fusion(bf16[512,4096]{1,0:T(8,128)(2,1)} %bitcast.22, s32[1024]{0:T(1024)S(1)} %pad_clamp_fusion), kind=kCustom, calls=%fused_computation | custom fusion | bytes 2097664 | tf_op jit(solution)/shard_map/jit(_take)/gather | solution.py:15
  175.9 3.3 gather.7
  179.2 2.4 fusion.6
  181.6 0.5 reshape.61
  182.0 2.0 scatter_custom_fusion.1
  184.0 2.7 reshape.38
  186.7 11.6 %all-to-all-start.1 = ((bf16[128,2,4096]{2,1,0:T(2,128)(2,1)}), bf16[128,2,4096]{2,1,0:T(2,128)(2,1)S(1)}, u32[]{:S(2)}, u32[]{:S(2)}) async-start(bf16[128,2,4096]{2,1,0:T(2,128)(2,1)} %reshape.38), calls=%async_computation.1 | async-start | bytes 4194304 | tf_op jit(solution)/shard_map/all_to_all | solution.py:42
  198.7 98.9 %all-to-all-done.1 = bf16[128,2,4096]{2,1,0:T(2,128)(2,1)S(1)} async-done(((bf16[128,2,4096]{2,1,0:T(2,128)(2,1)}), bf16[128,2,4096]{2,1,0:T(2,128)(2,1)S(1)}, u32[]{:S(2)}, u32[]{:S(2)}) %all-to-all-start.1) | async-done | bytes 2097184 | tf_op jit(solution)/shard_map/all_to_all | solution.py:42
  297.6 2.2 reshape.39
  299.9 2.7 fusion.14
  302.6 1.3 dynamic-slice
  304.5 48.7 %all-reduce.3.cloned.1.call-done = f32[16,4096]{1,0:T(8,128)} async-done(((f32[16,4096]{1,0:T(8,128)}), f32[16,4096]{1,0:T(8,128)}) %all-reduce.3.cloned.1.call-update) | async-done | bytes 262160
  353.2 1.6 fusion.12
  (17 shorter events, 0.6 us)
Async XLA Ops:
  6.5 28.7 %copy-start.1 = (s32[128]{0:T(128)S(1)}, s32[128]{0:T(128)}, u32[]{:S(2)}) copy-start(s32[128]{0:T(128)} %param.7) | copy-start | bytes 1540
  6.5 154.3 %all-gather.2.cloned.1.call-start = ((), (), s32[]{:S(2)}) async-start(), calls=%async_computation.2 | async-start | bytes 8454144 | tf_op jit(solution)/shard_map/all_gather | solution.py:14
  12.4 174.3 %all-to-all-start = ((bf16[128,1,2]{2,1,0:T(2,128)(2,1)}), bf16[128,1,2]{2,1,0:T(2,128)(2,1)S(1)}, u32[]{:S(2)}, u32[]{:S(2)}) async-start(bf16[128,1,2]{2,1,0:T(2,128)(2,1)} %all_to_all.12), calls=%async_computation | async-start | bytes 131072 | tf_op jit(solution)/shard_map/all_to_all | solution.py:49
  186.7 110.9 %all-to-all-start.1 = ((bf16[128,2,4096]{2,1,0:T(2,128)(2,1)}), bf16[128,2,4096]{2,1,0:T(2,128)(2,1)S(1)}, u32[]{:S(2)}, u32[]{:S(2)}) async-start(bf16[128,2,4096]{2,1,0:T(2,128)(2,1)} %reshape.38), calls=%async_computation.1 | async-start | bytes 4194304 | tf_op jit(solution)/shard_map/all_to_all | solution.py:42
  198.3 154.9 %all-reduce.3.cloned.1.call-start = ((), (), s32[]{:S(2)}) async-start(), calls=%async_computation.3 | async-start | bytes 524288
  299.8 53.4 %copy-start = (f32[1,4,4096]{2,1,0:T(4,128)S(1)}, f32[1,4,4096]{2,1,0:T(4,128)}, u32[]{:S(2)}) copy-start(f32[1,4,4096]{2,1,0:T(4,128)} %param.11) | copy-start | bytes 196612
Sparse Core Ops, SparseCore 0:
  10.5 150.3 all-gather.1
  302.7 50.4 all-reduce.2
where the time goes:
time: 362 us
  waiting for transfers between devices  273 us (75%)
  local copies, waits for them, and re-layouts  33.4 us (9%)
  starting transfers between devices  31.2 us (9%)
  between operations  14.2 us (4%)
  matrix products  5.09 us (1%)
  other arithmetic  4.7 us (1%)
    all_gather x1, waiting for transfers between devices, per_device(): gathered = lax.all_gather(amplitudes, 'rows', axis=1, tiled=True)[0]  125 us
    all_to_all x1, waiting for transfers between devices, per_device(): lax.all_to_all(outgoing.reshape(row_count, capacity, NIJ * TILE_SPAN), 'r...  98.9 us
    unnamed x3, waiting for transfers between devices  48.7 us
    all_to_all x1, starting transfers between devices, per_device(): lax.all_to_all(slot_ids.reshape(row_count, capacity), 'rows', split_axis=...  19.5 us
    unnamed x7, local copies, waits for them, and re-layouts  12.8 us
    all_to_all x1, starting transfers between devices, per_device(): lax.all_to_all(outgoing.reshape(row_count, capacity, NIJ * TILE_SPAN), 'r...  11.6 us
    gather x2, local copies, waits for them, and re-layouts, per_device(): jnp.take(gathered, integral_cd_tile, axis=0)  8.25 us
  transfers between devices with their start and end apart: 4, of which 3 were waited for; matrix products, arithmetic and copies ran while one was open for 10% of the time, Pallas kernels for 0%

commit v1 on v0

--- a/solution.py
+++ b/solution.py
@@ -11,7 +11,13 @@
 
 
 def per_device(tiles, integral_cd_tile, part_dest, partial_row_place, amplitudes, residual_in):
-    gathered = lax.all_gather(amplitudes, "rows", axis=1, tiled=True)[0]
+
+    def take_roots_here(page):
+        x_now = jnp.stack([page for _ in range(lax.axis_size("rows"))], axis=0)
+        value_now = lax.all_to_all(x_now, "rows", 0, 0)
+        return jnp.concatenate(value_now, 1)
+
+    gathered = take_roots_here(amplitudes)[0]
     picked = jnp.take(gathered, integral_cd_tile, axis=0).reshape(
         PAB, TILES_PER_PART, NIJ, TILE_SPAN
     )

time: 362 us -> 432 us (1.19)
  waiting for transfers between devices: 273 us -> 331 us
  starting transfers between devices: 31.2 us -> 46.2 us
    all_to_all x0 -> x1, waiting for transfers between devices: none -> 183 us  [take_roots_here(): value_now = lax.all_to_all(x_now, 'rows', 0, 0)]
    all_gather x1 -> x0, waiting for transfers between devices: 125 us -> none  [per_device(): gathered = lax.all_gather(amplitudes, 'rows', axis=1, tiled=True)[0]]
    all_to_all x0 -> x1, starting transfers between devices: none -> 20.1 us  [take_roots_here(): value_now = lax.all_to_all(x_now, 'rows', 0, 0)]
    another operation x0 -> x2, local copies, waits for them, and re-layouts: none -> 11.7 us  [the longest x1 6.91 us: per_device(): gathered = take_roots_here(amplitudes)[0]]
    unnamed x7 -> x11, local copies, waits for them, and re-layouts: 12.8 us -> 1.3 us
    all_to_all x1, starting transfers between devices: 19.5 us -> 9.86 us  [per_device(): lax.all_to_all(slot_ids.reshape(row_count, capacity), 'rows', split_axis=...]
    all_to_all x1, starting transfers between devices: 11.6 us -> 16.2 us  [per_device(): lax.all_to_all(outgoing.reshape(row_count, capacity, NIJ * TILE_SPAN), 'r...]
    unnamed x3 -> x2, waiting for transfers between devices: 48.7 us -> 48.9 us
  transfers between devices with their start and end apart: 4 -> 4, of which waited for: 3 -> 3; matrix products, arithmetic and copies ran while one was open for 10% -> 6% of each run, Pallas kernels for 0% -> 0%
where the time goes in v1:
time: 432 us; the launch traced here: 431 us
  waiting for transfers between devices  331 us (77%)
  starting transfers between devices  46.2 us (11%)
  local copies, waits for them, and re-layouts  32.6 us (8%)
  between operations  14.2 us (3%)
  matrix products  5.08 us (1%)
    all_to_all x1, waiting for transfers between devices, take_roots_here(): value_now = lax.all_to_all(x_now, 'rows', 0, 0)  183 us
    all_to_all x1, waiting for transfers between devices, per_device(): lax.all_to_all(outgoing.reshape(row_count, capacity, NIJ * TILE_SPAN), 'r...  98.9 us
    unnamed x2, waiting for transfers between devices  48.9 us
    all_to_all x1, starting transfers between devices, take_roots_here(): value_now = lax.all_to_all(x_now, 'rows', 0, 0)  20.1 us
    all_to_all x1, starting transfers between devices, per_device(): lax.all_to_all(outgoing.reshape(row_count, capacity, NIJ * TILE_SPAN), 'r...  16.2 us
    all_to_all x1, starting transfers between devices, per_device(): lax.all_to_all(slot_ids.reshape(row_count, capacity), 'rows', split_axis=...  9.86 us
  transfers between devices with their start and end apart: 4, of which 3 were waited for; matrix products, arithmetic and copies ran while one was open for 6% of the time, Pallas kernels for 0%

profile of v1, /device:TPU:2, one launch (start us, length us, event | category | flops | bytes accessed | tf_op | source)
XLA Modules:
  0.0 431.1 jit_solution(15949488717807850824)
XLA Ops:
  6.5 4.8 %stack.2 = bf16[128,1,4,4096]{3,2,1,0:T(4,128)(2,1)} broadcast(bf16[4,4096]{1,0:T(4,128)(2,1)} %bitcast.20), dimensions={2,3} | broadcast | bytes 4227072 | tf_op jit(solution)/shard_map/stack | solution.py:16
  11.4 20.1 %all-to-all-start.1 = ((bf16[128,1,4,4096]{3,2,1,0:T(4,128)(2,1)}), bf16[128,1,4,4096]{3,2,1,0:T(4,128)(2,1)}, u32[]{:S(2)}, u32[]{:S(2)}) async-start(bf16[128,1,4,4096]{3,2,1,0:T(4,128)(2,1)} %stack.2), calls=%async_computation.1 | async-start | bytes 8388608 | tf_op jit(solution)/shard_map/all_to_all | solution.py:17
  31.5 2.3 reshape.40
  34.1 0.2 select_reduce_fusion
  34.3 0.7 scatter_custom_fusion
  35.0 0.8 all_to_all.16
  35.8 183.2 %all-to-all-done.1 = bf16[128,1,4,4096]{3,2,1,0:T(4,128)(2,1)} async-done(((bf16[128,1,4,4096]{3,2,1,0:T(4,128)(2,1)}), bf16[128,1,4,4096]{3,2,1,0:T(4,128)(2,1)}, u32[]{:S(2)}, u32[]{:S(2)}) %all-to-all-start.1) | async-done | bytes 4194336 | tf_op jit(solution)/shard_map/all_to_all | solution.py:17
  219.0 9.9 %all-to-all-start = ((bf16[128,1,2]{2,1,0:T(2,128)(2,1)}), bf16[128,1,2]{2,1,0:T(2,128)(2,1)S(1)}, u32[]{:S(2)}, u32[]{:S(2)}) async-start(bf16[128,1,2]{2,1,0:T(2,128)(2,1)} %all_to_all.16), calls=%async_computation | async-start | bytes 131072 | tf_op jit(solution)/shard_map/all_to_all | solution.py:55
  228.9 6.9 %squeeze_reshape.3 = bf16[512,4096]{1,0:T(8,128)(2,1)} reshape(bf16[128,1,4,4096]{3,2,1,0:T(4,128)(2,1)} %all-to-all-done.1) | data formatting | bytes 8388608 | tf_op jit(solution)/shard_map/squeeze;reshape | solution.py:20
  235.8 4.9 %gather_fusion = bf16[128,4096]{1,0:T(8,128)(2,1)S(1)} fusion(bf16[512,4096]{1,0:T(8,128)(2,1)} %squeeze_reshape.3, s32[1024]{0:T(1024)S(1)} %pad_clamp_fusion), kind=kCustom, calls=%fused_computation | custom fusion | bytes 2097664 | tf_op jit(solution)/shard_map/jit(_take)/gather | solution.py:21
  240.7 3.3 gather.7
  244.0 2.3 fusion.6
  246.4 0.5 reshape.64
  246.9 2.0 scatter_custom_fusion.1
  248.8 2.7 reshape.41
  251.5 16.2 %all-to-all-start.2 = ((bf16[128,2,4096]{2,1,0:T(2,128)(2,1)}), bf16[128,2,4096]{2,1,0:T(2,128)(2,1)S(1)}, u32[]{:S(2)}, u32[]{:S(2)}) async-start(bf16[128,2,4096]{2,1,0:T(2,128)(2,1)} %reshape.41), calls=%async_computation.2 | async-start | bytes 4194304 | tf_op jit(solution)/shard_map/all_to_all | solution.py:48
  267.7 0.2 convert_reduce_fusion
  267.9 0.1 reshape.43
  268.1 98.9 %all-to-all-done.2 = bf16[128,2,4096]{2,1,0:T(2,128)(2,1)S(1)} async-done(((bf16[128,2,4096]{2,1,0:T(2,128)(2,1)}), bf16[128,2,4096]{2,1,0:T(2,128)(2,1)S(1)}, u32[]{:S(2)}, u32[]{:S(2)}) %all-to-all-start.2) | async-done | bytes 2097184 | tf_op jit(solution)/shard_map/all_to_all | solution.py:48
  367.0 2.2 reshape.42
  369.2 2.7 fusion.14
  371.9 1.3 dynamic-slice
  373.9 48.9 %all-reduce.3.cloned.1.call-done = f32[16,4096]{1,0:T(8,128)} async-done(((f32[16,4096]{1,0:T(8,128)}), f32[16,4096]{1,0:T(8,128)}) %all-reduce.3.cloned.1.call-update) | async-done | bytes 262160
  422.7 1.6 fusion.12
  (22 shorter events, 0.4 us)
Async XLA Ops:
  11.4 20.1 %copy-start = (bf16[128,4096]{1,0:T(8,128)(2,1)S(1)}, bf16[128,4096]{1,0:T(8,128)(2,1)}, u32[]{:S(2)}) copy-start(bf16[128,4096]{1,0:T(8,128)(2,1)} %param.6) | copy-start | bytes 3145732
  11.4 207.7 %all-to-all-start.1 = ((bf16[128,1,4,4096]{3,2,1,0:T(4,128)(2,1)}), bf16[128,1,4,4096]{3,2,1,0:T(4,128)(2,1)}, u32[]{:S(2)}, u32[]{:S(2)}) async-start(bf16[128,1,4,4096]{3,2,1,0:T(4,128)(2,1)} %stack.2), calls=%async_computation.1 | async-start | bytes 8388608 | tf_op jit(solution)/shard_map/all_to_all | solution.py:17
  31.5 2.3 copy-start.4
  31.5 2.5 copy-start.3
  31.5 2.5 copy-start.2
  219.0 32.5 %all-to-all-start = ((bf16[128,1,2]{2,1,0:T(2,128)(2,1)}), bf16[128,1,2]{2,1,0:T(2,128)(2,1)S(1)}, u32[]{:S(2)}, u32[]{:S(2)}) async-start(bf16[128,1,2]{2,1,0:T(2,128)(2,1)} %all_to_all.16), calls=%async_computation | async-start | bytes 131072 | tf_op jit(solution)/shard_map/all_to_all | solution.py:55
  251.5 115.5 %all-to-all-start.2 = ((bf16[128,2,4096]{2,1,0:T(2,128)(2,1)}), bf16[128,2,4096]{2,1,0:T(2,128)(2,1)S(1)}, u32[]{:S(2)}, u32[]{:S(2)}) async-start(bf16[128,2,4096]{2,1,0:T(2,128)(2,1)} %reshape.41), calls=%async_computation.2 | async-start | bytes 4194304 | tf_op jit(solution)/shard_map/all_to_all | solution.py:48
  267.7 155.0 %all-reduce.3.cloned.1.call-start = ((), (), s32[]{:S(2)}) async-start(), calls=%async_computation.3 | async-start | bytes 524288
  369.2 53.5 %copy-start.1 = (f32[1,4,4096]{2,1,0:T(4,128)S(1)}, f32[1,4,4096]{2,1,0:T(4,128)}, u32[]{:S(2)}) copy-start(f32[1,4,4096]{2,1,0:T(4,128)} %param.11) | copy-start | bytes 196612
Sparse Core Ops, SparseCore 0:
  372.1 50.6 all-reduce.2
